TPU v7x, 32 devices: a whole 2x2x4 slice. The times are simulated.
32 devices in a mesh: seq: 8 (over y, x, core), batch: 4 (over z).
Axes of the slice: x: 2, y: 2, z: 4, core: 2. Of those that a mesh axis runs over, the one named last changes fastest.
Arguments:
- tokens: bfloat16 [4, 4096, 2048], P('batch', 'seq'), may hold values from -6 to 6
- w_qkv: bfloat16 [2048, 3072], replicated, may hold values from -0.125 to 0.125
- cotangent: bfloat16 [4, 4096, 1024], P('batch', 'seq'), may hold values from -6 to 6
Outputs:
- attended: bfloat16 [4, 4096, 1024], P('batch', 'seq')
- token_grad: bfloat16 [4, 4096, 2048], P('batch', 'seq')
- weight_grad: float32 [2048, 3072], P('seq')
All inputs are finite; a program needn't handle non-finite values.
Results may differ from a plain program's by a relative error of at most 0.0064.
Values sent between devices are 32-bit elements; how exact they have to be, the bound alone decides.
A program may use at most 192 MiB of HBM per device.

v0:
```python
import functools

import jax
import jax.numpy as jnp
from jax import lax
from jax.experimental import pallas as pl
from jax.experimental.pallas import tpu as pltpu
from jax.sharding import PartitionSpec as P

HEADS = 8
DH = 128
BLK = 512


COLS = 128
MESH = pl.DeviceIdType.MESH


def bits_of(count):
    bits = count.bit_length() - 1
    assert count == 1 << bits
    return bits


def carries(own, seq_count, work):
    bits = bits_of(seq_count)
    rank = lax.axis_index("seq")
    half = own.shape[1] // 2

    def swap(value, bit):
        return lax.ppermute(value, "seq", [(i, i ^ (1 << bit)) for i in range(seq_count)])

    def sides(value, bit):
        upper = ((rank >> bit) & 1) == 1
        return jnp.stack([jnp.where(upper, value[0], 0.0), jnp.where(upper, 0.0, value[1])])

    other = swap(own, 0)
    near = sides(other, 0)
    total = lax.dynamic_slice_in_dim(own + other, (rank & 1) * half, half, 1)
    far = jnp.zeros_like(total)
    done = None
    for bit in range(1, bits):
        upper = ((rank >> bit) & 1) == 1
        last = bit == bits - 1
        other = swap(jnp.where(upper, total[1], total[0]) if last else total, bit)
        if bit == 1:
            done = work(total)
            other, done = lax.optimization_barrier((other, done))
        if last:
            far = far + jnp.stack([jnp.where(upper, other, 0.0), jnp.where(upper, 0.0, other)])
        else:
            far = far + sides(other, bit)
            total = total + other
    if done is None:
        done = work(total)
    mate = swap(far, 0)
    low = (rank & 1) == 0
    joined = jnp.concatenate([jnp.where(low, far, mate), jnp.where(low, mate, far)], 1)
    result = near + joined
    return result[0], result[1], done


def orders(bits):
    rest = list(range(1, bits))
    cut = len(rest) // 2
    return [[0] + rest, [0] + rest[cut:] + rest[:cut]]


def reduce_kernel(seq_count, batch_count, x_ref, g_ref, w_hbm, o_ref, t_ref, w_tiles, w_sem, mine, first, *rest):
    bits = bits_of(seq_count)
    lands = [first] + list(rest[: bits - 1])
    from_outer, from_inner, send_sem, recv_sem, z_send, z_recv = rest[bits - 1 :]
    chunks = mine.shape[0]
    half = mine.shape[1]
    own_rows = o_ref.shape[0]
    places = seq_count // 2
    order = orders(bits)
    rank = lax.axis_index("seq")
    plane = lax.axis_index("batch")
    middle = batch_count // 2
    low_side = plane < middle
    depth = jnp.where(low_side, middle - 1 - plane, plane - middle)
    has_outer = jnp.where(low_side, plane > 0, plane < batch_count - 1)
    is_inner = depth == 0
    inner = jnp.where(low_side, plane + 1, plane - 1)
    outer = jnp.where(low_side, plane - 1, plane + 1)

    barrier = pltpu.get_barrier_semaphore()
    for bit in range(bits):
        pl.semaphore_signal(barrier, inc=1, device_id={"seq": rank ^ (1 << bit)}, device_id_type=MESH)
    pl.semaphore_signal(barrier, inc=1, device_id={"batch": inner}, device_id_type=MESH)

    @pl.when(has_outer)
    def _():
        pl.semaphore_signal(barrier, inc=1, device_id={"batch": outer}, device_id_type=MESH)

    pl.semaphore_wait(barrier, bits + 1 + has_outer.astype(jnp.int32))

    def step_copy(chunk, step):
        size = half >> step
        source = mine.at[chunk] if step == 0 else first.at[chunk, pl.ds(size, size)]
        return pltpu.make_async_remote_copy(
            src_ref=source,
            dst_ref=lands[step].at[chunk],
            send_sem=send_sem.at[step, chunk],
            recv_sem=recv_sem.at[step, chunk],
            device_id={"seq": rank ^ (1 << order[chunk % 2][step])},
            device_id_type=MESH,
        )

    def inward(chunk, target):
        return pltpu.make_async_remote_copy(
            src_ref=first.at[chunk, pl.ds(0, own_rows)],
            dst_ref=target.at[chunk],
            send_sem=z_send.at[0, chunk],
            recv_sem=z_recv.at[0 if target is from_outer else 1, chunk],
            device_id={"batch": inner},
            device_id_type=MESH,
        )

    def outward(chunk):
        return pltpu.make_async_remote_copy(
            src_ref=from_inner.at[chunk],
            dst_ref=from_inner.at[chunk],
            send_sem=z_send.at[1, chunk],
            recv_sem=z_recv.at[1, chunk],
            device_id={"batch": outer},
            device_id_type=MESH,
        )

    def spots(owner_xor):
        return [
            sum((owner_xor // (1 << bit) % 2) * (1 << (bits - 1 - k)) for k, bit in enumerate(way) if k)
            for way in order
        ]

    def product(pair, owner_xor):
        owner = rank ^ owner_xor
        return jnp.dot(
            x_ref[pl.ds(pl.multiple_of(owner * own_rows, own_rows), own_rows), :],
            g_ref[:, pair * 2 * COLS : (pair + 1) * 2 * COLS],
            preferred_element_type=jnp.float32,
        )

    def open_pair(pair):
        @pl.loop(0, places)
        def _(index):
            value = product(pair, 2 * index + 1)
            for side, spot in enumerate(spots(2 * index + 1)):
                row = pl.multiple_of(spot * own_rows, own_rows)
                mine[2 * pair + side, pl.ds(row, own_rows), :] = value[:, side * COLS : (side + 1) * COLS]

        step_copy(2 * pair, 0).start()
        step_copy(2 * pair + 1, 0).start()

    def enter_pair(pair):
        step_copy(2 * pair, 0).wait_recv()
        step_copy(2 * pair + 1, 0).wait_recv()

        @pl.loop(0, places)
        def _(index):
            value = product(pair, 2 * index)
            for side, spot in enumerate(spots(2 * index)):
                row = pl.multiple_of(spot * own_rows, own_rows)
                first[2 * pair + side, pl.ds(row, own_rows), :] += value[:, side * COLS : (side + 1) * COLS]

        if bits > 1:
            step_copy(2 * pair, 1).start()
            step_copy(2 * pair + 1, 1).start()

    tile = w_tiles.shape[1]
    tiles = w_hbm.shape[0] // tile

    def w_copy(index):
        return pltpu.make_async_copy(
            w_hbm.at[pl.ds(index * tile, tile)], w_tiles.at[index % 2], w_sem.at[index % 2]
        )

    def token_tile(index):
        w_copy(index).wait()
        t_ref[:, index * tile : (index + 1) * tile] = lax.dot_general(
            g_ref[...], w_tiles[index % 2], (((1,), (1,)), ((), ())), preferred_element_type=jnp.float32
        ).astype(t_ref.dtype)
        if index + 2 < tiles:
            w_copy(index + 2).start()

    def halve(chunk, step):
        step_copy(chunk, step).wait_recv()
        size = half >> step
        first[chunk, pl.ds(0, size), :] += lands[step][chunk]
        if step + 1 < bits:
            step_copy(chunk, step + 1).start()

    def leave(chunk):
        @pl.when(jnp.logical_not(has_outer) & jnp.logical_not(is_inner))
        def _():
            inward(chunk, from_outer).start()

        @pl.when(jnp.logical_not(has_outer) & is_inner)
        def _():
            inward(chunk, from_inner).start()

    def gather(chunk):
        @pl.when(has_outer)
        def _():
            inward(chunk, from_outer).wait_recv()
            first[chunk, pl.ds(0, own_rows), :] += from_outer[chunk]

        @pl.when(has_outer & is_inner)
        def _():
            inward(chunk, from_inner).start()

        @pl.when(has_outer & jnp.logical_not(is_inner))
        def _():
            inward(chunk, from_outer).start()

    def close(chunk):
        inward(chunk, from_inner).wait_recv()

        @pl.when(is_inner)
        def _():
            from_inner[chunk] += first[chunk, pl.ds(0, own_rows), :]

        @pl.when(has_outer)
        def _():
            outward(chunk).start()

        o_ref[:, chunk * COLS : (chunk + 1) * COLS] = from_inner[chunk]

    stages = [functools.partial(halve, step=step) for step in range(1, bits)]
    stages += [leave, gather, close]
    lag = list(range(1, bits)) + [bits - 1, bits, bits + 1]
    pairs = chunks // 2
    ahead = 2
    for index in range(min(2, tiles)):
        w_copy(index).start()
    for pair in range(min(ahead, pairs)):
        open_pair(pair)
    for slot in range(pairs + lag[-1]):
        if slot < pairs:
            enter_pair(slot)
        if slot + ahead < pairs:
            open_pair(slot + ahead)
        for stage, late in zip(stages, lag):
            pair = slot - late
            if 0 <= pair < pairs:
                stage(2 * pair)
                stage(2 * pair + 1)
        if 1 <= slot <= tiles:
            token_tile(slot - 1)
    for index in range(pairs + lag[-1] - 1, tiles):
        token_tile(index)
    for chunk in range(chunks):
        for step in range(bits):
            step_copy(chunk, step).wait_send()
        inward(chunk, from_inner).wait_send()

        @pl.when(has_outer)
        def _():
            outward(chunk).wait_send()


def reduced_rows(local_x, qkv_grad, w_qkv, seq_count, batch_count):
    bits = bits_of(seq_count)
    positions, width = local_x.shape
    columns = qkv_grad.shape[1]
    chunks = columns // COLS
    half = width // 2
    own_rows = width // seq_count
    flops = 4 * positions * width * columns
    return pl.pallas_call(
        functools.partial(reduce_kernel, seq_count, batch_count),
        out_shape=(
            jax.ShapeDtypeStruct((own_rows, columns), jnp.float32),
            jax.ShapeDtypeStruct((positions, width), jnp.bfloat16),
        ),
        in_specs=[pl.BlockSpec(memory_space=pltpu.VMEM)] * 2 + [pl.BlockSpec(memory_space=pl.ANY)],
        out_specs=(pl.BlockSpec(memory_space=pltpu.VMEM), pl.BlockSpec(memory_space=pltpu.VMEM)),
        scratch_shapes=[
            pltpu.VMEM((2, 256, columns), jnp.bfloat16),
            pltpu.SemaphoreType.DMA((2,)),
            pltpu.VMEM((chunks, half, COLS), jnp.float32),
            pltpu.VMEM((chunks, half, COLS), jnp.float32),
            *[pltpu.VMEM((chunks, half >> step, COLS), jnp.float32) for step in range(1, bits)],
            pltpu.VMEM((chunks, own_rows, COLS), jnp.float32),
            pltpu.VMEM((chunks, own_rows, COLS), jnp.float32),
            pltpu.SemaphoreType.DMA((bits, chunks)),
            pltpu.SemaphoreType.DMA((bits, chunks)),
            pltpu.SemaphoreType.DMA((2, chunks)),
            pltpu.SemaphoreType.DMA((2, chunks)),
        ],
        compiler_params=pltpu.CompilerParams(
            collective_id=0, has_side_effects=True, vmem_limit_bytes=60 * 1024 * 1024
        ),
        cost_estimate=pl.CostEstimate(flops=flops, bytes_accessed=4 * width * columns, transcendentals=0),
    )(local_x.T, qkv_grad, w_qkv)


def dot(left, right, left_dim, right_dim):
    return lax.dot_general(
        left, right, (((left_dim,), (right_dim,)), ((), ())), preferred_element_type=jnp.float32
    )


def state_kernel(q_ref, k_ref, v_ref, c_ref, s_ref, g_ref, state_ref):
    grad = (c_ref[...].astype(jnp.float32) * s_ref[...]).astype(jnp.bfloat16)
    g_ref[...] = grad
    state_ref[0, 0] = dot(k_ref[...], v_ref[...], 0, 0)
    state_ref[1, 0] = dot(q_ref[...], grad, 0, 0)


def block_kernel(q_ref, k_ref, v_ref, g_ref, out_ref):
    query, key, value, grad = q_ref[...], k_ref[...], v_ref[...], g_ref[...]
    rows = lax.broadcasted_iota(jnp.int32, (BLK, BLK), 0)
    cols = lax.broadcasted_iota(jnp.int32, (BLK, BLK), 1)
    causal = rows >= cols
    scores = jnp.where(causal, dot(query, key, 1, 1), 0.0).astype(jnp.bfloat16)
    grad_scores = jnp.where(causal, dot(grad, value, 1, 1), 0.0).astype(jnp.bfloat16)
    out_ref[0] = dot(scores, value, 1, 0)
    out_ref[1] = dot(grad_scores, key, 1, 0)
    out_ref[2] = dot(grad_scores, query, 0, 0)
    out_ref[3] = dot(scores, grad, 0, 0)


def carry_kernel(q_ref, k_ref, v_ref, g_ref, s_ref, part_ref, kv_ref, gs_ref, a_ref, o_ref):
    head = pl.program_id(0)
    width = a_ref.shape[1] * pl.num_programs(0)

    def wide(left, state, state_dim):
        high = state.astype(jnp.bfloat16)
        rest = (state - high.astype(jnp.float32)).astype(jnp.bfloat16)
        return dot(left, high, 1, state_dim) + dot(left, rest, 1, state_dim)

    kv, grad_state = kv_ref[0], gs_ref[0]
    a_ref[...] = ((part_ref[0] + wide(q_ref[...], kv, 0)) * s_ref[...]).astype(a_ref.dtype)
    results = (
        part_ref[1] + wide(g_ref[...], kv, 1),
        part_ref[2] + wide(v_ref[...], grad_state, 1),
        part_ref[3] + wide(k_ref[...], grad_state, 0),
    )
    for index, result in enumerate(results):
        start = pl.multiple_of(index * width + head * DH, DH)
        o_ref[:, pl.ds(start, DH)] = result.astype(o_ref.dtype)


def body(tokens, w_qkv, cotangent):
    row_count = tokens.shape[1]
    width = w_qkv.shape[1] // 3
    assert row_count == BLK and width == HEADS * DH
    seq_count = lax.axis_size("seq")
    batch_count = lax.axis_size("batch")
    local_x = tokens[0]
    projected = jnp.dot(local_x, w_qkv, preferred_element_type=jnp.float32).astype(jnp.bfloat16)
    position = lax.axis_index("seq") * row_count + jnp.arange(row_count, dtype=jnp.int32)
    pos_scale = (DH ** (-0.5) / jnp.sqrt(position.astype(jnp.float32) + 1.0))[:, None]
    head_specs = [pl.BlockSpec((BLK, DH), lambda h, part=part: (0, part * HEADS + h)) for part in range(3)]
    own_spec = pl.BlockSpec((BLK, DH), lambda h: (0, h))
    scale_spec = pl.BlockSpec((BLK, 1), lambda h: (0, 0))
    part_spec = pl.BlockSpec((4, BLK, DH), lambda h: (0, 0, h))
    head_state = pl.BlockSpec((1, DH, DH), lambda h: (h, 0, 0))
    scaled_grad, states = pl.pallas_call(
        state_kernel,
        grid=(HEADS,),
        out_shape=(
            jax.ShapeDtypeStruct((row_count, width), jnp.bfloat16),
            jax.ShapeDtypeStruct((2, HEADS, DH, DH), jnp.float32),
        ),
        in_specs=head_specs + [own_spec, scale_spec],
        out_specs=(own_spec, pl.BlockSpec((2, 1, DH, DH), lambda h: (0, h, 0, 0))),
        cost_estimate=pl.CostEstimate(
            flops=4 * row_count * width * DH, bytes_accessed=10 * row_count * width, transcendentals=0
        ),
    )(projected, projected, projected, cotangent[0], pos_scale)
    in_block = pl.pallas_call(
        block_kernel,
        grid=(HEADS,),
        out_shape=jax.ShapeDtypeStruct((4, row_count, width), jnp.float32),
        in_specs=head_specs + [own_spec],
        out_specs=part_spec,
        cost_estimate=pl.CostEstimate(
            flops=12 * row_count * width * BLK, bytes_accessed=24 * row_count * width, transcendentals=0
        ),
    )

    def work(total):
        gated, _ = lax.optimization_barrier((scaled_grad, total))
        return in_block(projected, projected, projected, gated)

    kv_in, grad_in, parts = carries(states, seq_count, work)
    attended, qkv_grad = pl.pallas_call(
        carry_kernel,
        grid=(HEADS,),
        out_shape=(
            jax.ShapeDtypeStruct((row_count, width), jnp.bfloat16),
            jax.ShapeDtypeStruct((row_count, 3 * width), jnp.bfloat16),
        ),
        in_specs=head_specs + [own_spec, scale_spec, part_spec, head_state, head_state],
        out_specs=(own_spec, pl.BlockSpec((BLK, 3 * width), lambda h: (0, 0))),
        cost_estimate=pl.CostEstimate(
            flops=16 * row_count * width * DH, bytes_accessed=32 * row_count * width, transcendentals=0
        ),
    )(projected, projected, projected, scaled_grad, pos_scale, parts, kv_in, grad_in)
    summed, token_grad = reduced_rows(local_x, qkv_grad, w_qkv, seq_count, batch_count)
    grad_scale = 1.0 / jnp.sqrt(jnp.float32(batch_count * seq_count * row_count))
    weight_grad = summed * grad_scale
    return attended[None], token_grad[None], weight_grad


def solution(mesh):
    return jax.shard_map(
        body,
        mesh=mesh,
        in_specs=(P("batch", "seq", None), P(), P("batch", "seq", None)),
        out_specs=(P("batch", "seq", None), P("batch", "seq", None), P("seq", None)),
        check_vma=False,
    )
```

profile of v0, /device:TPU:0, one launch (start us, length us, event | category | flops | bytes accessed | tf_op | source)
XLA Modules:
  0.0 211.5 jit_solution(9917637954590215815)
XLA Ops:
  0.6 0.7 rsqrt_multiply_fusion.s_ref
  1.4 12.9 %convolution_convert_fusion.q_ref.k_ref.v_ref = bf16[512,3072]{1,0:T(8,128)(2,1)} fusion(bf16[2048,3072]{1,0:T(8,128)(2,1)} %w_hbm.1, bf16[1,512,2048]{2,1,0:T(8,128)(2,1)} %param.3), kind=kOutput, calls=%fused_computation | convolution fusion | flops 6444023808 | bytes 17825792 | tf_op jit(solution)/shard_map/dot_general | solution.py:353
  14.3 7.4 %shard_map.58 = (bf16[512,1024]{1,0:T(8,128)(2,1)}, f32[2,8,128,128]{3,2,1,0:T(8,128)}) custom-call(bf16[512,3072]{1,0:T(8,128)(2,1)} %convolution_convert_fusion.q_ref.k_ref.v_ref, bf16[512,3072]{1,0:T(8,128)(2,1)} %convolution_convert_fusion.q_ref.k_ref.v_ref, bf16[512,3072]{1,0:T(8,128)(2,1)} %convolution_convert_fusion.q_ref.k_ref.v_ref, ...), custom_call_target="tpu_custom_call" | custom-call | flops 268435456 | bytes 5242880 | tf_op jit(solution)/shard_map/pallas_call | solution.py:361
  21.7 0.5 collective-permute-start
  22.2 2.5 %collective-permute-done = f32[2,8,128,128]{3,2,1,0:T(8,128)S(1)} collective-permute-done((f32[2,8,128,128]{3,2,1,0:T(8,128)}, f32[2,8,128,128]{3,2,1,0:T(8,128)S(1)}, u32[]{:S(2)}, u32[]{:S(2)}) %collective-permute-start) | collective-permute-done | bytes 1048608 | tf_op jit(solution)/shard_map/ppermute | solution.py:31
  24.7 1.1 dynamic-slice_add_fusion
  25.8 2.9 %collective-permute-start.1 = (f32[2,4,128,128]{3,2,1,0:T(8,128)S(1)}, f32[2,4,128,128]{3,2,1,0:T(8,128)S(1)}, u32[]{:S(2)}, u32[]{:S(2)}) collective-permute-start(f32[2,4,128,128]{3,2,1,0:T(8,128)S(1)} %dynamic-slice_add_fusion), channel_id=1, source_target_pairs={{0,8},{4,12},{8,0},{12,4},{16,24},{20,28},{24,16},{28,20},{1,9},{5... | collective-permute-start | bytes 1572872 | tf_op jit(solution)/shard_map/ppermute | solution.py:31
  28.7 11.6 %shard_map.59.part_ref = f32[4,512,1024]{2,1,0:T(8,128)} custom-call(bf16[512,3072]{1,0:T(8,128)(2,1)} %convolution_convert_fusion.q_ref.k_ref.v_ref, bf16[512,3072]{1,0:T(8,128)(2,1)} %convolution_convert_fusion.q_ref.k_ref.v_ref, bf16[512,3072]{1,0:T(8,128)(2,1)} %convolution_convert_fusion.q_ref.k_ref.v_ref, bf16[512,1024]{1,0:T(8,128)(2,1)} %get-tuple-element.14.g_ref), custom_call_target="tpu_custom_call" | custom-call | flops 3221225472 | bytes 12582912 | tf_op jit(solution)/shard_map/pallas_call | solution.py:387
  40.3 0.6 collective-permute-done.1
  40.9 0.1 add.47
  41.0 1.8 collective-permute-start.2
  42.9 6.0 %collective-permute-done.2 = f32[4,128,128]{2,1,0:T(8,128)S(1)} collective-permute-done((f32[4,128,128]{2,1,0:T(8,128)S(1)}, f32[4,128,128]{2,1,0:T(8,128)S(1)}, u32[]{:S(2)}, u32[]{:S(2)}) %collective-permute-start.2) | collective-permute-done | bytes 262176 | tf_op jit(solution)/shard_map/ppermute | solution.py:31
  48.9 0.1 maximum_add_fusion.1
  49.0 0.1 collective-permute-start.3
  49.1 3.9 %copy.7 = bf16[1,512,2048]{1,2,0:T(8,128)(2,1)} copy(bf16[1,512,2048]{2,1,0:T(8,128)(2,1)} %param.3) | data formatting | bytes 4194304 | tf_op args[0]
  53.0 0.1 slice_select_fusion.1
  53.1 0.0 collective-permute-done.3
  53.1 0.1 broadcast_select_fusion.1
  53.2 0.1 maximum_add_fusion
  53.3 1.2 slice_bitcast_fusion
  54.5 10.7 %shard_map.60 = (bf16[512,1024]{1,0:T(8,128)(2,1)}, bf16[512,3072]{1,0:T(8,128)(2,1)}) custom-call(bf16[512,3072]{1,0:T(8,128)(2,1)} %convolution_convert_fusion.q_ref.k_ref.v_ref, bf16[512,3072]{1,0:T(8,128)(2,1)} %convolution_convert_fusion.q_ref.k_ref.v_ref, bf16[512,3072]{1,0:T(8,128)(2,1)} %convolution_convert_fusion.q_ref.k_ref.v_ref, ...), custom_call_target="tpu_custom_call" | custom-call | flops 1073741824 | bytes 16777216 | tf_op jit(solution)/shard_map/pallas_call | solution.py:390
  65.2 140.8 %shard_map.61 = (f32[256,3072]{1,0:T(8,128)}, bf16[512,2048]{1,0:T(8,128)(2,1)}) custom-call(bf16[2048,512]{1,0:T(8,128)(2,1)} %bitcast.20, bf16[512,3072]{1,0:T(8,128)(2,1)} %get-tuple-element.18.g_ref, bf16[2048,3072]{1,0:T(8,128)(2,1)} %w_hbm.1), custom_call_target="tpu_custom_call" | custom-call | flops 12884901888 | bytes 25165824 | tf_op jit(solution)/shard_map/pallas_call | solution.py:271
  206.1 0.0 copy-start
  206.1 4.1 %broadcast_multiply_fusion = f32[256,3072]{1,0:T(8,128)} fusion(f32[256,3072]{1,0:T(8,128)} %get-tuple-element.20), kind=kLoop, calls=%fused_computation.2 | loop fusion | flops 786432 | bytes 6291456 | tf_op jit(solution)/shard_map/mul | solution.py:405
  210.1 0.0 copy-done
  210.1 1.3 copy.10
  (3 shorter events, 0.1 us)
Async XLA Ops:
  21.7 3.0 %collective-permute-start = (f32[2,8,128,128]{3,2,1,0:T(8,128)}, f32[2,8,128,128]{3,2,1,0:T(8,128)S(1)}, u32[]{:S(2)}, u32[]{:S(2)}) collective-permute-start(f32[2,8,128,128]{3,2,1,0:T(8,128)} %get-tuple-element.13), channel_id=1, source_target_pairs={{0,4},{4,0},{8,12},{12,8},{16,20},{20,16},{24,28},{28,24},{1,5},{5... | collective-permute-start | bytes 3145736 | tf_op jit(solution)/shard_map/ppermute | solution.py:31
  25.8 15.1 %collective-permute-start.1 = (f32[2,4,128,128]{3,2,1,0:T(8,128)S(1)}, f32[2,4,128,128]{3,2,1,0:T(8,128)S(1)}, u32[]{:S(2)}, u32[]{:S(2)}) collective-permute-start(f32[2,4,128,128]{3,2,1,0:T(8,128)S(1)} %dynamic-slice_add_fusion), channel_id=1, source_target_pairs={{0,8},{4,12},{8,0},{12,4},{16,24},{20,28},{24,16},{28,20},{1,9},{5... | collective-permute-start | bytes 1572872 | tf_op jit(solution)/shard_map/ppermute | solution.py:31
  41.0 7.8 %collective-permute-start.2 = (f32[4,128,128]{2,1,0:T(8,128)S(1)}, f32[4,128,128]{2,1,0:T(8,128)S(1)}, u32[]{:S(2)}, u32[]{:S(2)}) collective-permute-start(f32[4,128,128]{2,1,0:T(8,128)S(1)} %fusion.1), channel_id=1, source_target_pairs={{0,16},{4,20},{8,24},{12,28},{16,0},{20,4},{24,8},{28,12},{1,17},{... | collective-permute-start | bytes 786440 | tf_op jit(solution)/shard_map/ppermute | solution.py:31
  49.0 4.1 %collective-permute-start.3 = (f32[2,4,128,128]{3,2,1,0:T(8,128)S(1)}, f32[2,4,128,128]{3,2,1,0:T(8,128)S(1)}, u32[]{:S(2)}, u32[]{:S(2)}) collective-permute-start(f32[2,4,128,128]{3,2,1,0:T(8,128)S(1)} %maximum_add_fusion.1), channel_id=1, source_target_pairs={{0,4},{4,0},{8,12},{12,8},{16,20},{20,16},{24,28},{28,24},{1,5},{5... | collective-permute-start | bytes 1572872 | tf_op jit(solution)/shard_map/ppermute | solution.py:31
  206.1 4.1 %copy-start = (bf16[512,2048]{1,0:T(8,128)(2,1)S(1)}, bf16[512,2048]{1,0:T(8,128)(2,1)}, u32[]{:S(2)}) copy-start(bf16[512,2048]{1,0:T(8,128)(2,1)} %get-tuple-element.19) | copy-start | bytes 6291460
where the time goes:
time: 212 us; the launch traced here: 211 us
  Pallas kernels  171 us (81%)
  matrix products  12.9 us (6%)
  waiting for transfers between devices  9.11 us (4%)
  other arithmetic  6.43 us (3%)
  local copies, waits for them, and re-layouts  6.4 us (3%)
  starting transfers between devices  5.31 us (3%)
    pallas_call x1, Pallas kernels, reduced_rows(): pl.pallas_call(functools.partial(reduce_kernel, seq_count, batch_count),...  141 us
    dot_general x1, matrix products, body(): jnp.dot(local_x, w_qkv, preferred_element_type=jnp.float32)  12.9 us
    pallas_call x1, Pallas kernels, work(): return in_block(projected, projected, projected, gated)  11.6 us
    pallas_call x1, Pallas kernels, body(): pl.pallas_call(carry_kernel, grid=(HEADS,), out_shape=(jax.ShapeDtypeStru...  10.7 us
    ppermute x4, waiting for transfers between devices, swap(): lax.ppermute(value, 'seq', [(i, i ^ 1 << bit) for i in range(seq_count)])  9.11 us
    pallas_call x1, Pallas kernels, body(): pl.pallas_call(state_kernel, grid=(HEADS,), out_shape=(jax.ShapeDtypeStru...  7.44 us
    ppermute x4, starting transfers between devices, swap(): lax.ppermute(value, 'seq', [(i, i ^ 1 << bit) for i in range(seq_count)])  5.31 us
    unnamed x4, local copies, waits for them, and re-layouts  5.25 us
  transfers between devices with their start and end apart: 4, of which 3 were waited for; matrix products, arithmetic and copies ran while one was open for 2% of the time, Pallas kernels for 5%

commit v1 on v0

v1 whole, which is shorter than its diff:
```python
import functools
import types

import jax
import jax.numpy as jnp
from jax import lax
from jax.experimental import pallas as pl
from jax.experimental.pallas import tpu as pltpu
from jax.sharding import PartitionSpec as P

HEADS = 8
DH = 128
BLK = 512
COLS = 128
PAIR = 2 * COLS
TILE = 256
MESH = pl.DeviceIdType.MESH
CROSS = ()


def bits_of(count):
    bits = count.bit_length() - 1
    assert count == 1 << bits
    return bits


def dot(left, right, left_dim, right_dim):
    return lax.dot_general(
        left, right, (((left_dim,), (right_dim,)), ((), ())), preferred_element_type=jnp.float32
    )


def wide(left, state, state_dim):
    high = state.astype(jnp.bfloat16)
    rest = (state - high.astype(jnp.float32)).astype(jnp.bfloat16)
    return dot(left, high, 1, state_dim) + dot(left, rest, 1, state_dim)


def lanes(start, size):
    return pl.ds(pl.multiple_of(start, COLS), size)


def step_kernel(seq_count, batch_count, grad_scale, names, x_hbm, w_hbm, c_hbm, a_hbm, t_hbm, o_hbm, *scratch):
    m = types.SimpleNamespace(**dict(zip(names, scratch)))
    bits = bits_of(seq_count) - 1
    chips = 1 << bits
    rows, width = x_hbm.shape
    head_width = c_hbm.shape[1]
    groups = head_width // PAIR
    pairs = 3 * groups
    chunks = 2 * pairs
    half = width // 2
    own_rows = width // seq_count
    rank = lax.axis_index("seq")
    core = rank % 2
    chip = rank // 2
    plane = lax.axis_index("batch")
    middle = batch_count // 2
    low_side = plane < middle
    depth = jnp.where(low_side, middle - 1 - plane, plane - middle)
    has_outer = jnp.where(low_side, plane > 0, plane < batch_count - 1)
    is_inner = depth == 0
    inner = jnp.where(low_side, plane + 1, plane - 1)
    outer = jnp.where(low_side, plane - 1, plane + 1)
    mate_id = {"seq": rank ^ 1}

    base = list(range(bits))
    turned = base[bits // 2 :] + base[: bits // 2]
    crossed = set(CROSS) if batch_count == 4 else set()
    ways = []
    for chunk in range(chunks):
        way = base if chunk % 2 == 0 else turned
        ways.append((["z"] if chunk // 2 in crossed else []) + way)
    cross_index = {chunk: i for i, chunk in enumerate(c for c in range(chunks) if c // 2 in crossed)}

    def local(source, target, sem):
        return pltpu.make_async_copy(source, target, sem)

    def remote(source, target, send, recv, device):
        return pltpu.make_async_remote_copy(
            src_ref=source, dst_ref=target, send_sem=send, recv_sem=recv, device_id=device, device_id_type=MESH
        )

    def w_part(group, part):
        column = lanes(part * head_width + group * PAIR, PAIR)
        return local(w_hbm.at[:, column], m.w_parts.at[part], m.w_sem.at[part])

    def w_tile(index):
        row = pl.ds(pl.multiple_of(index * TILE, TILE), TILE)
        return local(w_hbm.at[row], m.w_tiles.at[index % 2], m.t_sem.at[index % 2])

    def t_out(index):
        return local(m.t_tile.at[index % 2], t_hbm.at[:, lanes(index * TILE, TILE)], m.t_sem.at[2 + index % 2])

    def a_out(group):
        column = pl.ds(group * PAIR, PAIR)
        return local(m.grads.at[:, column], a_hbm.at[:, column], m.a_sem.at[group])

    def o_out(chunk):
        pair, side = chunk // 2, chunk % 2
        column = (pair % 3) * head_width + (pair // 3) * PAIR + side * COLS
        return local(m.from_inner.at[chunk], o_hbm.at[:, pl.ds(column, COLS)], m.o_sem.at[chunk])

    x_in = local(x_hbm, m.x_all, m.x_sem.at[0])
    c_in = local(c_hbm, m.grads, m.x_sem.at[1])
    for part in range(3):
        w_part(0, part).start()
        if part == 0:
            x_in.start()
    c_in.start()
    barrier = pltpu.get_barrier_semaphore()
    pl.semaphore_signal(barrier, inc=1, device_id=mate_id, device_id_type=MESH)
    for bit in range(bits):
        pl.semaphore_signal(barrier, inc=1, device_id={"seq": rank ^ (2 << bit)}, device_id_type=MESH)
    pl.semaphore_signal(barrier, inc=1, device_id={"batch": inner}, device_id_type=MESH)

    @pl.when(has_outer)
    def _():
        pl.semaphore_signal(barrier, inc=1, device_id={"batch": outer}, device_id_type=MESH)

    position = rank * rows + lax.broadcasted_iota(jnp.int32, (rows, COLS), 0)
    m.scale[...] = DH ** (-0.5) / jnp.sqrt(position.astype(jnp.float32) + 1.0)

    def project(group):
        @pl.loop(0, 3)
        def _(part):
            w_part(group, part).wait()
            m.qkv[:, lanes(part * head_width + group * PAIR, PAIR)] = dot(
                m.x_all[...], m.w_parts[part], 1, 0
            ).astype(m.qkv.dtype)
            if group + 1 < groups:
                w_part(group + 1, part).start()

    def head_columns(group, head):
        start = group * PAIR + head * DH
        return [lanes(part * head_width + start, DH) for part in range(3)] + [lanes(start, DH)]

    def first_swap(group):
        return remote(
            m.states.at[group, 1 - core], m.mates.at[group], m.swap_send.at[0, group], m.swap_recv.at[0, group], mate_id
        )

    def last_swap(group):
        return remote(
            m.gives.at[group], m.carry.at[group, core], m.swap_send.at[1, group], m.swap_recv.at[1, group], mate_id
        )

    def bit_swap(group, bit):
        return remote(
            m.totals.at[bit, group],
            m.others.at[bit, group],
            m.bit_send.at[bit, group],
            m.bit_recv.at[bit, group],
            {"seq": rank ^ (2 << bit)},
        )

    def takes(bit):
        return ((chip // (1 << bit)) % 2) != core

    def make_states(group):
        @pl.loop(0, 2)
        def _(head):
            q_at, k_at, v_at, g_at = head_columns(group, head)
            grad = (m.grads[:, g_at].astype(jnp.float32) * m.scale[...]).astype(jnp.bfloat16)
            m.grads[:, g_at] = grad
            m.states[group, 0, head] = dot(m.qkv[:, k_at], m.qkv[:, v_at], 0, 0)
            m.states[group, 1, head] = dot(m.qkv[:, q_at], grad, 0, 0)

        first_swap(group).start()

    def start_bit(group, bit):
        if bit == bits - 1:
            pl.when(jnp.logical_not(takes(bit)))(bit_swap(group, bit).start)
        else:
            bit_swap(group, bit).start()

    def chain_first(group):
        first_swap(group).wait_recv()
        m.totals[0, group] = m.states[group, core] + m.mates[group]
        start_bit(group, 0)
        m.carry[group, core] = jnp.zeros(m.mates.shape[1:], jnp.float32)

    def chain_bit(group, bit):
        last = bit == bits - 1
        if not last:
            bit_swap(group, bit).wait_recv()
            m.totals[bit + 1, group] = m.totals[bit, group] + m.others[bit, group]
            start_bit(group, bit + 1)

        @pl.when(takes(bit))
        def _():
            if last:
                bit_swap(group, bit).wait_recv()
            m.carry[group, core] += m.others[bit, group]

        if last:
            m.gives[group] = m.carry[group, core] + m.states[group, core]
            last_swap(group).start()

    chains = [
        [functools.partial(chain_first, group)] + [functools.partial(chain_bit, group, bit) for bit in range(bits)]
        for group in range(groups)
    ]

    def chain(group, count=None):
        count = len(chains[group]) if count is None else count
        for _ in range(min(count, len(chains[group]))):
            chains[group].pop(0)()

    def in_block(group):
        low = slice(0, TILE)
        high = slice(TILE, BLK)
        row = lax.broadcasted_iota(jnp.int32, (TILE, TILE), 0)
        col = lax.broadcasted_iota(jnp.int32, (TILE, TILE), 1)
        causal = row >= col

        @pl.loop(0, 2)
        def _(head):
            q_at, k_at, v_at, g_at = head_columns(group, head)
            out_at = lanes(head * DH, DH)

            def products(left_ref, left_at, right_at):
                def one(i, j, masked):
                    value = dot(left_ref[i, left_at], m.qkv[j, right_at], 1, 1)
                    if masked:
                        value = jnp.where(causal, value, 0.0)
                    return value.astype(jnp.bfloat16)

                m.tri[0] = one(low, low, True)
                m.tri[1] = one(high, low, False)
                m.tri[2] = one(high, high, True)

            def by_rows(index, ref, at):
                m.parts[index, low, out_at] = dot(m.tri[0], ref[low, at], 1, 0)
                m.parts[index, high, out_at] = dot(m.tri[1], ref[low, at], 1, 0) + dot(m.tri[2], ref[high, at], 1, 0)

            def by_columns(index, ref, at):
                m.parts[index, low, out_at] = dot(m.tri[0], ref[low, at], 0, 0) + dot(m.tri[1], ref[high, at], 0, 0)
                m.parts[index, high, out_at] = dot(m.tri[2], ref[high, at], 0, 0)

            products(m.qkv, q_at, k_at)
            by_rows(0, m.qkv, v_at)
            by_columns(3, m.grads, g_at)
            products(m.grads, g_at, v_at)
            by_rows(1, m.qkv, k_at)
            by_columns(2, m.qkv, q_at)

    def grad_swap(group, part):
        slot = group % 2
        return remote(
            m.g_send.at[slot, part],
            m.g_land.at[slot, part],
            m.g_ssem.at[group, part],
            m.g_rsem.at[group, part],
            mate_id,
        )

    def finish(group):
        slot = group % 2
        last_swap(group).wait_recv()
        if group >= 2:
            for part in range(3):
                grad_swap(group - 2, part).wait_send()

        @pl.loop(0, 2)
        def _(head):
            q_at, k_at, v_at, g_at = head_columns(group, head)
            out_at = lanes(head * DH, DH)
            query, key, value, grad = m.qkv[:, q_at], m.qkv[:, k_at], m.qkv[:, v_at], m.grads[:, g_at]
            kv, gs = m.carry[group, 0, head], m.carry[group, 1, head]
            attended = (m.parts[0, :, out_at] + wide(query, kv, 0)) * m.scale[...]
            results = (
                m.parts[1, :, out_at] + wide(grad, kv, 1),
                m.parts[2, :, out_at] + wide(value, gs, 1),
                m.parts[3, :, out_at] + wide(key, gs, 0),
            )
            m.grads[:, g_at] = attended.astype(jnp.bfloat16)
            for part, at in enumerate((q_at, k_at, v_at)):
                low = results[part].astype(jnp.bfloat16)
                m.qkv[:, at] = low
                m.g_cat[part, 0:rows, out_at] = low
                m.g_send[slot, part, head] = low.astype(jnp.float32)

        for part in range(3):
            grad_swap(group, part).start()
        a_out(group).start()

    spare = rows // COLS
    x_swap = remote(
        m.mine.at[pl.ds(chunks - spare, spare)],
        m.mine.at[pl.ds(chunks - 2 * spare, spare)],
        m.x_sem.at[2],
        m.x_sem.at[3],
        mate_id,
    )

    def turn_tokens():
        @pl.loop(0, chips)
        def _(index):
            owner = chip ^ index
            m.turned[...] = m.x_all[:, lanes(owner * 2 * own_rows, 2 * own_rows)].T
            row = pl.ds(pl.multiple_of(index * own_rows, own_rows), own_rows)
            m.x_cat[row, 0:rows] = m.turned[pl.ds(pl.multiple_of(core * own_rows, own_rows), own_rows), :]
            other = m.turned[pl.ds(pl.multiple_of((1 - core) * own_rows, own_rows), own_rows), :]
            for piece in range(spare):
                m.mine[chunks - spare + piece, row, :] = other[:, piece * COLS : (piece + 1) * COLS].astype(jnp.float32)

        x_swap.start()

    def join_tokens():
        x_swap.wait_recv()
        for piece in range(spare):
            at = rows + piece * COLS
            m.x_cat[:, at : at + COLS] = m.mine[chunks - 2 * spare + piece].astype(jnp.bfloat16)

    keeps_low = jnp.where(is_inner, 0, 1)

    def multiply(pair):
        group, part = pair // 3, pair % 3
        grad_swap(group, part).wait_recv()
        for side in range(2):
            m.g_cat[part, rows : 2 * rows, side * COLS : (side + 1) * COLS] = m.g_land[group % 2, part, side].astype(
                jnp.bfloat16
            )
        if group == groups - 1 and part == 0:
            x_swap.wait_send()

        @pl.loop(0, chips)
        def _(index):
            value = dot(
                m.x_cat[pl.ds(pl.multiple_of(index * own_rows, own_rows), own_rows), :], m.g_cat[part], 1, 0
            )
            for side in range(2):
                chunk = 2 * pair + side
                way = [bit for bit in ways[chunk] if bit != "z"]
                spot = sum((index // (1 << bit) % 2) * (1 << (bits - 1 - k)) for k, bit in enumerate(way))
                piece = value[:, side * COLS : (side + 1) * COLS]
                if chunk in cross_index:
                    part_rows = own_rows // 2
                    for low in range(2):
                        far = keeps_low if low else 1 - keeps_low
                        row = pl.multiple_of((far * chips + spot) * part_rows, part_rows)
                        m.mine[chunk, pl.ds(row, part_rows), :] = piece[low * part_rows : (low + 1) * part_rows]
                else:
                    row = pl.multiple_of(spot * own_rows, own_rows)
                    m.mine[chunk, pl.ds(row, own_rows), :] = piece

    def step_copy(chunk, step):
        size = half >> (step + 1)
        way = ways[chunk][step]
        land = m.lands[step].at[cross_index[chunk] if step == bits else chunk]
        device = {"batch": plane ^ 1} if way == "z" else {"seq": rank ^ (2 << way)}
        return remote(
            m.mine.at[chunk, pl.ds(size, size)], land, m.step_send.at[step, chunk], m.step_recv.at[step, chunk], device
        )

    def kept_rows(chunk):
        return own_rows // 2 if chunk in cross_index else own_rows

    def inward(chunk, to_inner):
        if to_inner:
            target = m.from_inner.at[chunk]
        else:
            target = m.from_outer.at[chunk, pl.ds(0, kept_rows(chunk))]
        return target

    def inward_copy(chunk, leaf, to_inner):
        source = m.mine.at[chunk, pl.ds(0, kept_rows(chunk))] if leaf else m.from_outer.at[chunk]
        return remote(
            source,
            inward(chunk, to_inner),
            m.z_send.at[0, chunk],
            m.z_recv.at[1 if to_inner else 0, chunk],
            {"batch": inner},
        )

    def outward(chunk):
        return remote(
            m.from_inner.at[chunk], m.from_inner.at[chunk], m.z_send.at[1, chunk], m.z_recv.at[1, chunk], {"batch": outer}
        )

    lone = batch_count == 2

    def leave(chunk):
        @pl.when(jnp.logical_not(has_outer))
        def _():
            inward_copy(chunk, True, lone).start()

    def halve(chunk, step):
        step_copy(chunk, step).wait_recv()
        size = half >> (step + 1)
        land = m.lands[step].at[cross_index[chunk] if step == bits else chunk]
        if step + 1 < len(ways[chunk]):
            part = size // 2
            m.mine[chunk, pl.ds(part, part), :] += land[pl.ds(part, part), :]
            step_copy(chunk, step + 1).start()
            m.mine[chunk, pl.ds(0, part), :] += land[pl.ds(0, part), :]
        else:
            m.mine[chunk, pl.ds(0, size), :] += land[...]
            leave(chunk)

    def gather(chunk):
        if lone:
            return

        @pl.when(has_outer)
        def _():
            inward_copy(chunk, True, False).wait_recv()
            kept = kept_rows(chunk)
            if chunk in cross_index:
                m.from_outer[chunk, pl.ds(kept, kept), :] = m.mine[chunk, pl.ds(0, kept), :]
            else:
                m.from_outer[chunk] += m.mine[chunk, pl.ds(0, kept), :]

        @pl.when(has_outer & is_inner)
        def _():
            inward_copy(chunk, False, True).start()

        if batch_count > 4:

            @pl.when(has_outer & jnp.logical_not(is_inner))
            def _():
                inward_copy(chunk, False, False).start()

    def close(chunk):
        inward_copy(chunk, lone, True).wait_recv()

        @pl.when(is_inner)
        def _():
            own = m.mine[chunk, pl.ds(0, own_rows), :] if lone else m.from_outer[chunk]
            m.from_inner[chunk] = (m.from_inner[chunk] + own) * grad_scale

        @pl.when(has_outer)
        def _():
            outward(chunk).start()

        o_out(chunk).start()

    tiles = width // TILE

    def token_tiles(first, count):
        @pl.loop(first, first + count)
        def _(index):
            w_tile(index).wait()

            @pl.when(index >= 2)
            def _():
                t_out(index - 2).wait()

            m.t_tile[index % 2] = dot(m.qkv[...], m.w_tiles[index % 2], 1, 1).astype(m.t_tile.dtype)
            t_out(index).start()

            @pl.when(index + 2 < tiles)
            def _():
                w_tile(index + 2).start()

    def open_pair(pair):
        for chunk in (2 * pair, 2 * pair + 1):
            step_copy(chunk, 0).start()

    events = {}
    for pair in range(pairs):
        for chunk in (2 * pair, 2 * pair + 1):
            count = len(ways[chunk])
            for step in range(count):
                events.setdefault(pair + step, []).append((-step, chunk, functools.partial(halve, chunk, step)))
            events.setdefault(pair + count, []).append((-count, chunk, functools.partial(gather, chunk)))
            events.setdefault(pair + count + 1, []).append((-count - 1, chunk, functools.partial(close, chunk)))

    def run_events(slot):
        for _, _, event in sorted(events.get(slot, []), key=lambda item: item[:2]):
            event()

    x_in.wait()
    project(0)
    c_in.wait()
    pl.semaphore_wait(barrier, bits + 2 + has_outer.astype(jnp.int32))
    make_states(0)
    turn_tokens()
    chain(0, 1)
    project(1)
    chain(0, 1)
    make_states(1)
    in_block(0)
    chain(0)
    chain(1, 1)
    join_tokens()
    finish(0)
    in_block(1)
    chain(1, 1)
    for pair in range(3):
        multiply(pair)
        if pair < 2:
            open_pair(pair)
    for index in range(2):
        w_tile(index).start()

    chain(1)
    finish(1)
    project(2)
    make_states(2)
    per_slot = {
        0: [lambda: multiply(3), lambda: chain(2, 1), lambda: multiply(4), lambda: project(3)],
        1: [lambda: multiply(5), lambda: make_states(3), lambda: chain(2, 1)],
        2: [lambda: in_block(2), lambda: chain(2), lambda: chain(3, 1)],
        3: [lambda: finish(2), lambda: in_block(3), lambda: multiply(6)],
        4: [lambda: multiply(7), lambda: chain(3, 1), lambda: multiply(8)],
        5: [lambda: chain(3), lambda: finish(3)],
        6: [lambda: multiply(9), lambda: multiply(10)],
        7: [lambda: multiply(11)],
    }
    for index in range(tiles // 2):
        per_slot.setdefault(8 + index, []).append(functools.partial(token_tiles, 2 * index, 2))
    for slot in range(max(max(events), max(per_slot)) + 1):
        run_events(slot)
        if slot + 2 < pairs:
            open_pair(slot + 2)
        for task in per_slot.get(slot, []):
            task()

    x_swap_pending = groups < 1
    assert not x_swap_pending
    for index in range(tiles - 2, tiles):
        t_out(index).wait()
    for group in range(groups):
        a_out(group).wait()
        first_swap(group).wait_send()
        last_swap(group).wait_send()
        for bit in range(bits):
            if bit == bits - 1:
                pl.when(jnp.logical_not(takes(bit)))(bit_swap(group, bit).wait_send)
            else:
                bit_swap(group, bit).wait_send()
        if group >= groups - 2:
            for part in range(3):
                grad_swap(group, part).wait_send()
    for chunk in range(chunks):
        for step in range(len(ways[chunk])):
            step_copy(chunk, step).wait_send()
        if lone:
            inward_copy(chunk, True, True).wait_send()
        else:

            @pl.when(jnp.logical_not(has_outer))
            def _():
                inward_copy(chunk, True, False).wait_send()

            @pl.when(has_outer)
            def _():
                inward_copy(chunk, False, True).wait_send()
                outward(chunk).wait_send()

        o_out(chunk).wait()


def body(tokens, w_qkv, cotangent):
    rows, width = tokens.shape[1:]
    columns = w_qkv.shape[1]
    head_width = columns // 3
    assert rows == BLK and head_width == HEADS * DH
    seq_count = lax.axis_size("seq")
    batch_count = lax.axis_size("batch")
    bits = bits_of(seq_count) - 1
    groups = head_width // PAIR
    chunks = columns // COLS
    half = width // 2
    own_rows = width // seq_count
    crossed = 2 * len(CROSS)
    grad_scale = float(batch_count * seq_count * rows) ** -0.5
    f32, bf16 = jnp.float32, jnp.bfloat16
    state = (2, DH, DH)
    sizes = dict(
        x_all=pltpu.VMEM((rows, width), bf16),
        x_cat=pltpu.VMEM((half, 2 * rows), bf16),
        turned=pltpu.VMEM((2 * own_rows, rows), bf16),
        w_parts=pltpu.VMEM((3, width, PAIR), bf16),
        w_tiles=pltpu.VMEM((2, TILE, columns), bf16),
        t_tile=pltpu.VMEM((2, rows, TILE), bf16),
        qkv=pltpu.VMEM((rows, columns), bf16),
        grads=pltpu.VMEM((rows, head_width), bf16),
        scale=pltpu.VMEM((rows, COLS), f32),
        parts=pltpu.VMEM((4, rows, PAIR), f32),
        tri=pltpu.VMEM((3, TILE, TILE), bf16),
        states=pltpu.VMEM((groups, 2) + state, f32),
        mates=pltpu.VMEM((groups,) + state, f32),
        gives=pltpu.VMEM((groups,) + state, f32),
        totals=pltpu.VMEM((bits, groups) + state, f32),
        others=pltpu.VMEM((bits, groups) + state, f32),
        carry=pltpu.VMEM((groups, 2) + state, f32),
        g_send=pltpu.VMEM((2, 3, 2, rows, COLS), f32),
        g_land=pltpu.VMEM((2, 3, 2, rows, COLS), f32),
        g_cat=pltpu.VMEM((3, 2 * rows, PAIR), bf16),
        mine=pltpu.VMEM((chunks, half, COLS), f32),
        lands=[pltpu.VMEM((chunks, half >> (step + 1), COLS), f32) for step in range(bits)]
        + [pltpu.VMEM((max(crossed, 1), half >> (bits + 1), COLS), f32)],
        from_outer=pltpu.VMEM((chunks, own_rows, COLS), f32),
        from_inner=pltpu.VMEM((chunks, own_rows, COLS), f32),
        w_sem=pltpu.SemaphoreType.DMA((3,)),
        x_sem=pltpu.SemaphoreType.DMA((4,)),
        t_sem=pltpu.SemaphoreType.DMA((4,)),
        a_sem=pltpu.SemaphoreType.DMA((groups,)),
        o_sem=pltpu.SemaphoreType.DMA((chunks,)),
        swap_send=pltpu.SemaphoreType.DMA((2, groups)),
        swap_recv=pltpu.SemaphoreType.DMA((2, groups)),
        bit_send=pltpu.SemaphoreType.DMA((bits, groups)),
        bit_recv=pltpu.SemaphoreType.DMA((bits, groups)),
        g_ssem=pltpu.SemaphoreType.DMA((groups, 3)),
        g_rsem=pltpu.SemaphoreType.DMA((groups, 3)),
        step_send=pltpu.SemaphoreType.DMA((bits + 1, chunks)),
        step_recv=pltpu.SemaphoreType.DMA((bits + 1, chunks)),
        z_send=pltpu.SemaphoreType.DMA((2, chunks)),
        z_recv=pltpu.SemaphoreType.DMA((2, chunks)),
    )
    attended, token_grad, weight_grad = pl.pallas_call(
        functools.partial(step_kernel, seq_count, batch_count, grad_scale, tuple(sizes)),
        out_shape=(
            jax.ShapeDtypeStruct((rows, head_width), bf16),
            jax.ShapeDtypeStruct((rows, width), bf16),
            jax.ShapeDtypeStruct((own_rows, columns), f32),
        ),
        in_specs=[pl.BlockSpec(memory_space=pl.ANY)] * 3,
        out_specs=[pl.BlockSpec(memory_space=pl.ANY)] * 3,
        scratch_shapes=list(sizes.values()),
        compiler_params=pltpu.CompilerParams(
            collective_id=0, has_side_effects=True, vmem_limit_bytes=62 * 1024 * 1024
        ),
    )(tokens[0], w_qkv, cotangent[0])
    return attended[None], token_grad[None], weight_grad


def solution(mesh):
    return jax.shard_map(
        body,
        mesh=mesh,
        in_specs=(P("batch", "seq", None), P(), P("batch", "seq", None)),
        out_specs=(P("batch", "seq", None), P("batch", "seq", None), P("seq", None)),
        check_vma=False,
    )
```

time: 212 us -> 165 us (0.78)
  Pallas kernels: 171 us -> 158 us
  matrix products: 12.9 us -> 0 us
  waiting for transfers between devices: 9.11 us -> 0 us
  other arithmetic: 6.43 us -> 0 us
  starting transfers between devices: 5.31 us -> 0 us
    dot_general x1 -> x0, matrix products: 12.9 us -> none  [body(): jnp.dot(local_x, w_qkv, preferred_element_type=jnp.float32)]
    pallas_call x4 -> x1, Pallas kernels: 171 us -> 158 us  [body(): pl.pallas_call(functools.partial(step_kernel, seq_count, batch_count, gra...]
    ppermute x4 -> x0, waiting for transfers between devices: 9.11 us -> none  [swap(): lax.ppermute(value, 'seq', [(i, i ^ 1 << bit) for i in range(seq_count)])]
    ppermute x4 -> x0, starting transfers between devices: 5.31 us -> none  [swap(): lax.ppermute(value, 'seq', [(i, i ^ 1 << bit) for i in range(seq_count)])]
    mul x1 -> x0, other arithmetic: 4.05 us -> none  [body(): weight_grad = summed * grad_scale]
    unnamed x4 -> x7, local copies, waits for them, and re-layouts: 5.25 us -> 5.41 us
  transfers between devices with their start and end apart: 4 -> 0, of which waited for: 3 -> 0; matrix products, arithmetic and copies ran while one was open for 2% -> 0% of each run, Pallas kernels for 5% -> 0%
where the time goes in v1:
time: 165 us; the launch traced here: 164 us
  Pallas kernels  158 us (96%)
  local copies, waits for them, and re-layouts  5.41 us (3%)
    pallas_call x1, Pallas kernels, body(): pl.pallas_call(functools.partial(step_kernel, seq_count, batch_count, gra...  158 us
    unnamed x7, local copies, waits for them, and re-layouts  5.41 us

profile of v1, /device:TPU:0, one launch (start us, length us, event | category | flops | bytes accessed | tf_op | source)
XLA Modules:
  0.0 164.3 jit_solution(16409099699976794045)
XLA Ops:
  0.6 158.2 %shard_map.58 = (bf16[512,1024]{1,0:T(8,128)(2,1)}, bf16[512,2048]{1,0:T(8,128)(2,1)}, f32[256,3072]{1,0:T(8,128)}) custom-call(bf16[512,2048]{1,0:T(8,128)(2,1)} %bitcast.4, bf16[2048,3072]{1,0:T(8,128)(2,1)} %w_hbm.1, bf16[512,1024]{1,0:T(8,128)(2,1)} %bitcast.7), custom_call_target="tpu_custom_call" | custom-call | tf_op jit(solution)/shard_map/pallas_call | solution.py:614
  158.9 0.0 copy-start.1
  158.9 0.0 copy-start
  158.9 2.4 %copy.9 = bf16[1,512,1024]{2,1,0:T(8,128)(2,1)} copy(bf16[1,512,1024]{2,1,0:T(8,128)(2,1)} %bitcast.6) | data formatting | bytes 2097152
  161.3 0.0 copy-done.1
  161.3 1.3 copy.10
  162.6 0.0 copy-done
  162.6 1.7 %copy.11 = f32[256,3072]{1,0:T(8,128)} copy(f32[256,3072]{1,0:T(8,128)S(1)} %copy-done) | data formatting | bytes 6291456
Async XLA Ops:
  158.9 2.4 %copy-start.1 = (bf16[512,2048]{1,0:T(8,128)(2,1)S(1)}, bf16[512,2048]{1,0:T(8,128)(2,1)}, u32[]{:S(2)}) copy-start(bf16[512,2048]{1,0:T(8,128)(2,1)} %get-tuple-element.7) | copy-start | bytes 6291460
  158.9 3.7 %copy-start = (f32[256,3072]{1,0:T(8,128)S(1)}, f32[256,3072]{1,0:T(8,128)}, u32[]{:S(2)}) copy-start(f32[256,3072]{1,0:T(8,128)} %get-tuple-element.14) | copy-start | bytes 9437188

commit v2 on v1

--- a/solution.py
+++ b/solution.py
@@ -15,7 +15,14 @@
 PAIR = 2 * COLS
 TILE = 256
 MESH = pl.DeviceIdType.MESH
-CROSS = ()
+CROSS = (2, 5)
+SEQUENCE = (0, 1, 3, 2, 4, 5, 6, 7, 8, 9, 10, 11)
+PLACES = 6
+SPLIT = {10: 2, 11: 2}
+EARLY = 4
+EARLY_LAGS = (1, 2, 3)
+MID_LAGS = (0, 1, 2)
+LAST_LAGS = (0, 2, 4)
 
 
 def bits_of(count):
@@ -66,12 +73,34 @@
 
     base = list(range(bits))
     turned = base[bits // 2 :] + base[: bits // 2]
+    ways = [base, turned]
     crossed = set(CROSS) if batch_count == 4 else set()
-    ways = []
-    for chunk in range(chunks):
-        way = base if chunk % 2 == 0 else turned
-        ways.append((["z"] if chunk // 2 in crossed else []) + way)
-    cross_index = {chunk: i for i, chunk in enumerate(c for c in range(chunks) if c // 2 in crossed)}
+    assert sorted(SEQUENCE) == list(range(pairs))
+    places = [(pair, sub) for pair in SEQUENCE for sub in range(SPLIT.get(pair, 1))]
+
+    def units_of(position):
+        pair, sub = places[position]
+        count = SPLIT.get(pair, 1)
+        return [
+            types.SimpleNamespace(
+                position=position,
+                chunk=2 * pair + side,
+                side=side,
+                sub=sub,
+                count=count,
+                crossed=pair in crossed,
+                place=(position % PLACES) * 2 + side,
+                kept=own_rows // 2 if pair in crossed else own_rows // count,
+                rows=pl.ds(sub * (own_rows // count), own_rows // count),
+                first=sub * (own_rows // count),
+            )
+            for side in range(2)
+        ]
+
+    def earlier(unit):
+        if unit.position < PLACES:
+            return None
+        return units_of(unit.position - PLACES)[unit.side]
 
     def local(source, target, sem):
         return pltpu.make_async_copy(source, target, sem)
@@ -96,10 +125,11 @@
         column = pl.ds(group * PAIR, PAIR)
         return local(m.grads.at[:, column], a_hbm.at[:, column], m.a_sem.at[group])
 
-    def o_out(chunk):
-        pair, side = chunk // 2, chunk % 2
-        column = (pair % 3) * head_width + (pair // 3) * PAIR + side * COLS
-        return local(m.from_inner.at[chunk], o_hbm.at[:, pl.ds(column, COLS)], m.o_sem.at[chunk])
+    def o_out(unit):
+        group, spot = unit.chunk // 6, unit.chunk % 6
+        column = (spot % 3) * head_width + group * PAIR + (spot // 3) * COLS
+        row = unit.rows
+        return local(m.from_inner.at[unit.chunk, row], o_hbm.at[row, pl.ds(column, COLS)], m.o_sem.at[unit.place])
 
     x_in = local(x_hbm, m.x_all, m.x_sem.at[0])
     c_in = local(c_hbm, m.grads, m.x_sem.at[1])
@@ -207,14 +237,14 @@
         for _ in range(min(count, len(chains[group]))):
             chains[group].pop(0)()
 
-    def in_block(group):
+    def in_block(group, first=0, count=2):
         low = slice(0, TILE)
         high = slice(TILE, BLK)
         row = lax.broadcasted_iota(jnp.int32, (TILE, TILE), 0)
         col = lax.broadcasted_iota(jnp.int32, (TILE, TILE), 1)
         causal = row >= col
 
-        @pl.loop(0, 2)
+        @pl.loop(first, first + count)
         def _(head):
             q_at, k_at, v_at, g_at = head_columns(group, head)
             out_at = lanes(head * DH, DH)
@@ -245,22 +275,19 @@
             by_rows(1, m.qkv, k_at)
             by_columns(2, m.qkv, q_at)
 
-    def grad_swap(group, part):
+    def grad_swap(group, spot):
         slot = group % 2
         return remote(
-            m.g_send.at[slot, part],
-            m.g_land.at[slot, part],
-            m.g_ssem.at[group, part],
-            m.g_rsem.at[group, part],
+            m.g_send.at[slot, spot],
+            m.g_land.at[slot, spot],
+            m.g_ssem.at[slot, spot],
+            m.g_rsem.at[slot, spot],
             mate_id,
         )
 
     def finish(group):
         slot = group % 2
         last_swap(group).wait_recv()
-        if group >= 2:
-            for part in range(3):
-                grad_swap(group - 2, part).wait_send()
 
         @pl.loop(0, 2)
         def _(head):
@@ -268,34 +295,39 @@
             out_at = lanes(head * DH, DH)
             query, key, value, grad = m.qkv[:, q_at], m.qkv[:, k_at], m.qkv[:, v_at], m.grads[:, g_at]
             kv, gs = m.carry[group, 0, head], m.carry[group, 1, head]
+
+            def give(part, at, result):
+                spot = 3 * head + part
+                low = result.astype(jnp.bfloat16)
+                m.qkv[:, at] = low
+                m.g_cat[spot // 2, 0:rows, lanes(spot % 2 * COLS, COLS)] = low
+                if group >= 2:
+                    grad_swap(group - 2, spot).wait_send()
+                m.g_send[slot, spot] = low.astype(jnp.float32)
+                grad_swap(group, spot).start()
+
+            give(0, q_at, m.parts[1, :, out_at] + wide(grad, kv, 1))
+            give(1, k_at, m.parts[2, :, out_at] + wide(value, gs, 1))
+            give(2, v_at, m.parts[3, :, out_at] + wide(key, gs, 0))
             attended = (m.parts[0, :, out_at] + wide(query, kv, 0)) * m.scale[...]
-            results = (
-                m.parts[1, :, out_at] + wide(grad, kv, 1),
-                m.parts[2, :, out_at] + wide(value, gs, 1),
-                m.parts[3, :, out_at] + wide(key, gs, 0),
-            )
             m.grads[:, g_at] = attended.astype(jnp.bfloat16)
-            for part, at in enumerate((q_at, k_at, v_at)):
-                low = results[part].astype(jnp.bfloat16)
-                m.qkv[:, at] = low
-                m.g_cat[part, 0:rows, out_at] = low
-                m.g_send[slot, part, head] = low.astype(jnp.float32)
-
-        for part in range(3):
-            grad_swap(group, part).start()
+
         a_out(group).start()
 
     spare = rows // COLS
-    x_swap = remote(
-        m.mine.at[pl.ds(chunks - spare, spare)],
-        m.mine.at[pl.ds(chunks - 2 * spare, spare)],
-        m.x_sem.at[2],
-        m.x_sem.at[3],
-        mate_id,
-    )
-
-    def turn_tokens():
-        @pl.loop(0, chips)
+
+    def x_swap(index):
+        row = pl.ds(pl.multiple_of(index * own_rows, own_rows), own_rows)
+        return remote(
+            m.mine.at[pl.ds(chunks - spare, spare), row],
+            m.mine.at[pl.ds(chunks - 2 * spare, spare), row],
+            m.x_send.at[index],
+            m.x_recv.at[index],
+            mate_id,
+        )
+
+    def turn_tokens(first, last):
+        @pl.loop(first, last)
         def _(index):
             owner = chip ^ index
             m.turned[...] = m.x_all[:, lanes(owner * 2 * own_rows, 2 * own_rows)].T
@@ -304,137 +336,202 @@
             other = m.turned[pl.ds(pl.multiple_of((1 - core) * own_rows, own_rows), own_rows), :]
             for piece in range(spare):
                 m.mine[chunks - spare + piece, row, :] = other[:, piece * COLS : (piece + 1) * COLS].astype(jnp.float32)
-
-        x_swap.start()
+            x_swap(index).start()
 
     def join_tokens():
-        x_swap.wait_recv()
-        for piece in range(spare):
-            at = rows + piece * COLS
-            m.x_cat[:, at : at + COLS] = m.mine[chunks - 2 * spare + piece].astype(jnp.bfloat16)
+        @pl.loop(0, chips)
+        def _(index):
+            x_swap(index).wait_recv()
+            row = pl.ds(pl.multiple_of(index * own_rows, own_rows), own_rows)
+            for piece in range(spare):
+                at = rows + piece * COLS
+                m.x_cat[row, at : at + COLS] = m.mine[chunks - 2 * spare + piece, row, :].astype(jnp.bfloat16)
 
     keeps_low = jnp.where(is_inner, 0, 1)
 
+    ready = set()
+
     def multiply(pair):
-        group, part = pair // 3, pair % 3
-        grad_swap(group, part).wait_recv()
+        group = pair // 3
+        ready.add(pair)
         for side in range(2):
-            m.g_cat[part, rows : 2 * rows, side * COLS : (side + 1) * COLS] = m.g_land[group % 2, part, side].astype(
+            spot = 2 * (pair % 3) + side
+            grad_swap(group, spot).wait_recv()
+            m.g_cat[spot // 2, rows : 2 * rows, side * COLS : (side + 1) * COLS] = m.g_land[group % 2, spot].astype(
                 jnp.bfloat16
             )
-        if group == groups - 1 and part == 0:
-            x_swap.wait_send()
+        if pair == (chunks - spare) // 2:
+            for index in range(chips):
+                x_swap(index).wait_send()
+        count = 2 if pair in crossed else SPLIT.get(pair, 1)
 
         @pl.loop(0, chips)
         def _(index):
             value = dot(
-                m.x_cat[pl.ds(pl.multiple_of(index * own_rows, own_rows), own_rows), :], m.g_cat[part], 1, 0
+                m.x_cat[pl.ds(pl.multiple_of(index * own_rows, own_rows), own_rows), :], m.g_cat[pair % 3], 1, 0
             )
-            for side in range(2):
-                chunk = 2 * pair + side
-                way = [bit for bit in ways[chunk] if bit != "z"]
+            for side, way in enumerate(ways):
                 spot = sum((index // (1 << bit) % 2) * (1 << (bits - 1 - k)) for k, bit in enumerate(way))
-                piece = value[:, side * COLS : (side + 1) * COLS]
-                if chunk in cross_index:
-                    part_rows = own_rows // 2
-                    for low in range(2):
-                        far = keeps_low if low else 1 - keeps_low
-                        row = pl.multiple_of((far * chips + spot) * part_rows, part_rows)
-                        m.mine[chunk, pl.ds(row, part_rows), :] = piece[low * part_rows : (low + 1) * part_rows]
-                else:
-                    row = pl.multiple_of(spot * own_rows, own_rows)
-                    m.mine[chunk, pl.ds(row, own_rows), :] = piece
-
-    def step_copy(chunk, step):
-        size = half >> (step + 1)
-        way = ways[chunk][step]
-        land = m.lands[step].at[cross_index[chunk] if step == bits else chunk]
-        device = {"batch": plane ^ 1} if way == "z" else {"seq": rank ^ (2 << way)}
+                part_rows = own_rows // count
+                for sub in range(count):
+                    block = sub
+                    if pair in crossed:
+                        block = 1 - keeps_low if sub == 0 else keeps_low
+                    row = pl.multiple_of((block * chips + spot) * part_rows, part_rows)
+                    m.mine[2 * pair + side, pl.ds(row, part_rows), :] = value[
+                        sub * part_rows : (sub + 1) * part_rows, side * COLS : (side + 1) * COLS
+                    ]
+
+        if pair in crossed:
+            for unit in units_of(places.index((pair, 0))):
+                cross_copy(unit).start()
+
+    def cross_copy(unit):
+        index = CROSS.index(unit.chunk // 2) * 2 + unit.side
         return remote(
-            m.mine.at[chunk, pl.ds(size, size)], land, m.step_send.at[step, chunk], m.step_recv.at[step, chunk], device
-        )
-
-    def kept_rows(chunk):
-        return own_rows // 2 if chunk in cross_index else own_rows
-
-    def inward(chunk, to_inner):
+            m.mine.at[unit.chunk, pl.ds(half // 2, half // 2)],
+            m.cross_land.at[index],
+            m.cross_send.at[index],
+            m.cross_recv.at[index],
+            {"batch": plane ^ 1},
+        )
+
+    def step_size(unit, step):
+        whole = half // 2 if unit.crossed else half // unit.count
+        return whole >> (step + 1), unit.sub * whole
+
+    def landing(unit, step):
+        size, _ = step_size(unit, step)
+        return m.lands[step].at[unit.place, pl.ds(0, size)]
+
+    def step_copy(unit, step):
+        size, start = step_size(unit, step)
+        return remote(
+            m.mine.at[unit.chunk, pl.ds(start + size, size)],
+            landing(unit, step),
+            m.step_send.at[step, unit.place],
+            m.step_recv.at[step, unit.place],
+            {"seq": rank ^ (2 << ways[unit.side][step])},
+        )
+
+    def start_step(unit, step):
+        before = earlier(unit)
+        if before is not None:
+            step_copy(before, step).wait_send()
+        step_copy(unit, step).start()
+
+    lone = batch_count == 2
+
+    def inward_copy(unit, leaf, to_inner):
+        _, start = step_size(unit, 0)
+        if leaf:
+            source = m.mine.at[unit.chunk, pl.ds(start, unit.kept)]
+        else:
+            source = m.from_outer.at[unit.chunk, unit.rows]
         if to_inner:
-            target = m.from_inner.at[chunk]
+            target = m.from_inner.at[unit.chunk, unit.rows]
         else:
-            target = m.from_outer.at[chunk, pl.ds(0, kept_rows(chunk))]
-        return target
-
-    def inward_copy(chunk, leaf, to_inner):
-        source = m.mine.at[chunk, pl.ds(0, kept_rows(chunk))] if leaf else m.from_outer.at[chunk]
+            target = m.from_outer.at[unit.chunk, pl.ds(unit.first, unit.kept)]
         return remote(
             source,
-            inward(chunk, to_inner),
-            m.z_send.at[0, chunk],
-            m.z_recv.at[1 if to_inner else 0, chunk],
+            target,
+            m.z_send.at[0, unit.place],
+            m.z_recv.at[1 if to_inner else 0, unit.place],
             {"batch": inner},
         )
 
-    def outward(chunk):
-        return remote(
-            m.from_inner.at[chunk], m.from_inner.at[chunk], m.z_send.at[1, chunk], m.z_recv.at[1, chunk], {"batch": outer}
-        )
-
-    lone = batch_count == 2
-
-    def leave(chunk):
+    def outward(unit):
+        both = m.from_inner.at[unit.chunk, unit.rows]
+        return remote(both, both, m.z_send.at[1, unit.place], m.z_recv.at[1, unit.place], {"batch": outer})
+
+    def start_inward(unit, leaf, to_inner):
+        before = earlier(unit)
+        if before is not None:
+            inward_copy(before, leaf, to_inner).wait_send()
+        inward_copy(unit, leaf, to_inner).start()
+
+    def leave(unit):
         @pl.when(jnp.logical_not(has_outer))
         def _():
-            inward_copy(chunk, True, lone).start()
-
-    def halve(chunk, step):
-        step_copy(chunk, step).wait_recv()
-        size = half >> (step + 1)
-        land = m.lands[step].at[cross_index[chunk] if step == bits else chunk]
-        if step + 1 < len(ways[chunk]):
+            start_inward(unit, True, lone)
+
+    def halve(unit, step):
+        step_copy(unit, step).wait_recv()
+        size, start = step_size(unit, step)
+        land = landing(unit, step)
+        if step + 1 < bits:
             part = size // 2
-            m.mine[chunk, pl.ds(part, part), :] += land[pl.ds(part, part), :]
-            step_copy(chunk, step + 1).start()
-            m.mine[chunk, pl.ds(0, part), :] += land[pl.ds(0, part), :]
+            m.mine[unit.chunk, pl.ds(start + part, part), :] += land[pl.ds(part, part), :]
+            start_step(unit, step + 1)
+            m.mine[unit.chunk, pl.ds(start, part), :] += land[pl.ds(0, part), :]
         else:
-            m.mine[chunk, pl.ds(0, size), :] += land[...]
-            leave(chunk)
-
-    def gather(chunk):
+            m.mine[unit.chunk, pl.ds(start, size), :] += land[...]
+            leave(unit)
+
+    def gather(unit):
         if lone:
             return
+        _, start = step_size(unit, 0)
+        kept = unit.kept
 
         @pl.when(has_outer)
         def _():
-            inward_copy(chunk, True, False).wait_recv()
-            kept = kept_rows(chunk)
-            if chunk in cross_index:
-                m.from_outer[chunk, pl.ds(kept, kept), :] = m.mine[chunk, pl.ds(0, kept), :]
+            inward_copy(unit, True, False).wait_recv()
+            if unit.crossed:
+                m.from_outer[unit.chunk, pl.ds(kept, kept), :] = m.mine[unit.chunk, pl.ds(start, kept), :]
             else:
-                m.from_outer[chunk] += m.mine[chunk, pl.ds(0, kept), :]
+                m.from_outer[unit.chunk, pl.ds(unit.first, kept), :] += m.mine[unit.chunk, pl.ds(start, kept), :]
 
         @pl.when(has_outer & is_inner)
         def _():
-            inward_copy(chunk, False, True).start()
+            start_inward(unit, False, True)
 
         if batch_count > 4:
 
             @pl.when(has_outer & jnp.logical_not(is_inner))
             def _():
-                inward_copy(chunk, False, False).start()
-
-    def close(chunk):
-        inward_copy(chunk, lone, True).wait_recv()
+                start_inward(unit, False, False)
+
+    def write_out(unit):
+        before = earlier(unit)
+        if before is not None:
+            o_out(before).wait()
+        o_out(unit).start()
+
+    def close(unit):
+        row = unit.rows
+        before = earlier(unit)
 
         @pl.when(is_inner)
         def _():
-            own = m.mine[chunk, pl.ds(0, own_rows), :] if lone else m.from_outer[chunk]
-            m.from_inner[chunk] = (m.from_inner[chunk] + own) * grad_scale
-
-        @pl.when(has_outer)
+            inward_copy(unit, lone, True).wait_recv()
+            own = m.mine[unit.chunk, row, :] if lone else m.from_outer[unit.chunk, row, :]
+            m.from_inner[unit.chunk, row, :] = (m.from_inner[unit.chunk, row, :] + own) * grad_scale
+
+        @pl.when(is_inner & has_outer)
         def _():
-            outward(chunk).start()
-
-        o_out(chunk).start()
+            if before is not None:
+                outward(before).wait_send()
+            outward(unit).start()
+
+        pl.when(is_inner)(lambda: write_out(unit))
+
+    def take(unit):
+        before = earlier(unit)
+
+        @pl.when(jnp.logical_not(is_inner))
+        def _():
+            inward_copy(unit, lone, True).wait_recv()
+
+        if batch_count > 4:
+
+            @pl.when(jnp.logical_not(is_inner) & has_outer)
+            def _():
+                if before is not None:
+                    outward(before).wait_send()
+                outward(unit).start()
+
+        pl.when(jnp.logical_not(is_inner))(lambda: write_out(unit))
 
     tiles = width // TILE
 
@@ -454,21 +551,35 @@
             def _():
                 w_tile(index + 2).start()
 
-    def open_pair(pair):
-        for chunk in (2 * pair, 2 * pair + 1):
-            step_copy(chunk, 0).start()
+    def open_place(position):
+        assert places[position][0] in ready
+        for unit in units_of(position):
+            if unit.crossed:
+                cross_copy(unit).wait_recv()
+                index = CROSS.index(unit.chunk // 2) * 2 + unit.side
+                part = half // 4
+                upper = pl.ds(part, part)
+                m.mine[unit.chunk, upper, :] += m.cross_land[index, upper, :]
+                start_step(unit, 0)
+                lower = pl.ds(0, part)
+                m.mine[unit.chunk, lower, :] += m.cross_land[index, lower, :]
+            else:
+                start_step(unit, 0)
 
     events = {}
-    for pair in range(pairs):
-        for chunk in (2 * pair, 2 * pair + 1):
-            count = len(ways[chunk])
-            for step in range(count):
-                events.setdefault(pair + step, []).append((-step, chunk, functools.partial(halve, chunk, step)))
-            events.setdefault(pair + count, []).append((-count, chunk, functools.partial(gather, chunk)))
-            events.setdefault(pair + count + 1, []).append((-count - 1, chunk, functools.partial(close, chunk)))
+    for position in range(len(places)):
+        for order, unit in enumerate(units_of(position)):
+            stages = [functools.partial(halve, unit, step) for step in range(bits)]
+            for number, stage in enumerate(stages):
+                events.setdefault(position + number, []).append((0, -number, order, stage))
+            late = EARLY_LAGS if position < EARLY else (MID_LAGS if unit.count == 1 else LAST_LAGS)
+            for number, (stage, lag) in enumerate(zip((gather, close, take), late)):
+                events.setdefault(position + bits + lag, []).append(
+                    (1, -number, order, functools.partial(stage, unit))
+                )
 
     def run_events(slot):
-        for _, _, event in sorted(events.get(slot, []), key=lambda item: item[:2]):
+        for _, _, _, event in sorted(events.get(slot, []), key=lambda item: item[:3]):
             event()
 
     x_in.wait()
@@ -476,50 +587,64 @@
     c_in.wait()
     pl.semaphore_wait(barrier, bits + 2 + has_outer.astype(jnp.int32))
     make_states(0)
-    turn_tokens()
+    turn_tokens(0, 1)
     chain(0, 1)
+    turn_tokens(1, chips)
     project(1)
+    make_states(1)
+    in_block(0, 0, 1)
     chain(0, 1)
-    make_states(1)
-    in_block(0)
+    in_block(0, 1, 1)
+    chain(1, 1)
     chain(0)
+    finish(0)
+    join_tokens()
     chain(1, 1)
-    join_tokens()
-    finish(0)
-    in_block(1)
-    chain(1, 1)
-    for pair in range(3):
-        multiply(pair)
-        if pair < 2:
-            open_pair(pair)
+    multiply(0)
+    open_place(0)
+    multiply(1)
+    open_place(1)
+    multiply(2)
+    chain(1)
     for index in range(2):
         w_tile(index).start()
-
-    chain(1)
-    finish(1)
-    project(2)
-    make_states(2)
-    per_slot = {
-        0: [lambda: multiply(3), lambda: chain(2, 1), lambda: multiply(4), lambda: project(3)],
-        1: [lambda: multiply(5), lambda: make_states(3), lambda: chain(2, 1)],
-        2: [lambda: in_block(2), lambda: chain(2), lambda: chain(3, 1)],
+    for group in (2, 3):
+        project(group)
+        make_states(group)
+    chain(2, 1)
+    chain(3, 1)
+    ahead = {
+        1: [
+            lambda: in_block(1),
+            lambda: finish(1),
+            lambda: multiply(3),
+            lambda: open_place(2),
+            lambda: multiply(4),
+            lambda: multiply(5),
+        ],
+    }
+    opens = {0: [], 1: [3]}
+    after = {
+        1: [lambda: in_block(2), lambda: chain(2, 1), lambda: chain(3, 1)],
+        2: [lambda: chain(2), lambda: chain(3)],
         3: [lambda: finish(2), lambda: in_block(3), lambda: multiply(6)],
-        4: [lambda: multiply(7), lambda: chain(3, 1), lambda: multiply(8)],
-        5: [lambda: chain(3), lambda: finish(3)],
+        4: [lambda: multiply(7), lambda: multiply(8)],
+        5: [lambda: finish(3)],
         6: [lambda: multiply(9), lambda: multiply(10)],
         7: [lambda: multiply(11)],
     }
     for index in range(tiles // 2):
-        per_slot.setdefault(8 + index, []).append(functools.partial(token_tiles, 2 * index, 2))
-    for slot in range(max(max(events), max(per_slot)) + 1):
+        after.setdefault(8 + index, []).append(functools.partial(token_tiles, 2 * index, 2))
+    for slot in range(max(max(events), max(after)) + 1):
+        for task in ahead.get(slot, []):
+            task()
         run_events(slot)
-        if slot + 2 < pairs:
-            open_pair(slot + 2)
-        for task in per_slot.get(slot, []):
+        for position in opens.get(slot, [slot + 2]):
+            if position < len(places):
+                open_place(position)
+        for task in after.get(slot, []):
             task()
 
-    x_swap_pending = groups < 1
-    assert not x_swap_pending
     for index in range(tiles - 2, tiles):
         t_out(index).wait()
     for group in range(groups):
@@ -532,25 +657,39 @@
             else:
                 bit_swap(group, bit).wait_send()
         if group >= groups - 2:
-            for part in range(3):
-                grad_swap(group, part).wait_send()
-    for chunk in range(chunks):
-        for step in range(len(ways[chunk])):
-            step_copy(chunk, step).wait_send()
-        if lone:
-            inward_copy(chunk, True, True).wait_send()
-        else:
-
-            @pl.when(jnp.logical_not(has_outer))
-            def _():
-                inward_copy(chunk, True, False).wait_send()
-
-            @pl.when(has_outer)
-            def _():
-                inward_copy(chunk, False, True).wait_send()
-                outward(chunk).wait_send()
-
-        o_out(chunk).wait()
+            for spot in range(6):
+                grad_swap(group, spot).wait_send()
+    for position in range(len(places)):
+        for unit in units_of(position):
+            if unit.crossed:
+                cross_copy(unit).wait_send()
+            if position < len(places) - PLACES:
+                continue
+            for step in range(bits):
+                step_copy(unit, step).wait_send()
+            if lone:
+                inward_copy(unit, True, True).wait_send()
+            else:
+
+                @pl.when(jnp.logical_not(has_outer))
+                def _():
+                    inward_copy(unit, True, False).wait_send()
+
+                @pl.when(has_outer & is_inner)
+                def _():
+                    inward_copy(unit, False, True).wait_send()
+
+                if batch_count > 4:
+
+                    @pl.when(has_outer & jnp.logical_not(is_inner))
+                    def _():
+                        inward_copy(unit, False, False).wait_send()
+
+                @pl.when(has_outer)
+                def _():
+                    outward(unit).wait_send()
+
+            o_out(unit).wait()
 
 
 def body(tokens, w_qkv, cotangent):
@@ -565,7 +704,8 @@
     chunks = columns // COLS
     half = width // 2
     own_rows = width // seq_count
-    crossed = 2 * len(CROSS)
+    crossed = max(2 * len(CROSS), 1)
+    places = 2 * PLACES
     grad_scale = float(batch_count * seq_count * rows) ** -0.5
     f32, bf16 = jnp.float32, jnp.bfloat16
     state = (2, DH, DH)
@@ -587,29 +727,33 @@
         totals=pltpu.VMEM((bits, groups) + state, f32),
         others=pltpu.VMEM((bits, groups) + state, f32),
         carry=pltpu.VMEM((groups, 2) + state, f32),
-        g_send=pltpu.VMEM((2, 3, 2, rows, COLS), f32),
-        g_land=pltpu.VMEM((2, 3, 2, rows, COLS), f32),
+        g_send=pltpu.VMEM((2, 6, rows, COLS), f32),
+        g_land=pltpu.VMEM((2, 6, rows, COLS), f32),
         g_cat=pltpu.VMEM((3, 2 * rows, PAIR), bf16),
         mine=pltpu.VMEM((chunks, half, COLS), f32),
-        lands=[pltpu.VMEM((chunks, half >> (step + 1), COLS), f32) for step in range(bits)]
-        + [pltpu.VMEM((max(crossed, 1), half >> (bits + 1), COLS), f32)],
+        lands=[pltpu.VMEM((places, half >> (step + 1), COLS), f32) for step in range(bits)],
+        cross_land=pltpu.VMEM((crossed, half // 2, COLS), f32),
         from_outer=pltpu.VMEM((chunks, own_rows, COLS), f32),
         from_inner=pltpu.VMEM((chunks, own_rows, COLS), f32),
         w_sem=pltpu.SemaphoreType.DMA((3,)),
-        x_sem=pltpu.SemaphoreType.DMA((4,)),
+        x_sem=pltpu.SemaphoreType.DMA((2,)),
+        x_send=pltpu.SemaphoreType.DMA((1 << bits,)),
+        x_recv=pltpu.SemaphoreType.DMA((1 << bits,)),
         t_sem=pltpu.SemaphoreType.DMA((4,)),
         a_sem=pltpu.SemaphoreType.DMA((groups,)),
-        o_sem=pltpu.SemaphoreType.DMA((chunks,)),
+        o_sem=pltpu.SemaphoreType.DMA((places,)),
         swap_send=pltpu.SemaphoreType.DMA((2, groups)),
         swap_recv=pltpu.SemaphoreType.DMA((2, groups)),
         bit_send=pltpu.SemaphoreType.DMA((bits, groups)),
         bit_recv=pltpu.SemaphoreType.DMA((bits, groups)),
-        g_ssem=pltpu.SemaphoreType.DMA((groups, 3)),
-        g_rsem=pltpu.SemaphoreType.DMA((groups, 3)),
-        step_send=pltpu.SemaphoreType.DMA((bits + 1, chunks)),
-        step_recv=pltpu.SemaphoreType.DMA((bits + 1, chunks)),
-        z_send=pltpu.SemaphoreType.DMA((2, chunks)),
-        z_recv=pltpu.SemaphoreType.DMA((2, chunks)),
+        g_ssem=pltpu.SemaphoreType.DMA((2, 6)),
+        g_rsem=pltpu.SemaphoreType.DMA((2, 6)),
+        cross_send=pltpu.SemaphoreType.DMA((crossed,)),
+        cross_recv=pltpu.SemaphoreType.DMA((crossed,)),
+        step_send=pltpu.SemaphoreType.DMA((bits, places)),
+        step_recv=pltpu.SemaphoreType.DMA((bits, places)),
+        z_send=pltpu.SemaphoreType.DMA((2, places)),
+        z_recv=pltpu.SemaphoreType.DMA((2, places)),
     )
     attended, token_grad, weight_grad = pl.pallas_call(
         functools.partial(step_kernel, seq_count, batch_count, grad_scale, tuple(sizes)),
@@ -622,7 +766,7 @@
         out_specs=[pl.BlockSpec(memory_space=pl.ANY)] * 3,
         scratch_shapes=list(sizes.values()),
         compiler_params=pltpu.CompilerParams(
-            collective_id=0, has_side_effects=True, vmem_limit_bytes=62 * 1024 * 1024
+            collective_id=0, has_side_effects=True, vmem_limit_bytes=60 * 1024 * 1024
         ),
     )(tokens[0], w_qkv, cotangent[0])
     return attended[None], token_grad[None], weight_grad

time: 165 us -> 149 us (0.903)
  Pallas kernels: 158 us -> 142 us
    pallas_call x1, Pallas kernels: 158 us -> 142 us  [body(): pl.pallas_call(functools.partial(step_kernel, seq_count, batch_count, gra...]
where the time goes in v2:
time: 149 us; the launch traced here: 148 us
  Pallas kernels  142 us (95%)
  local copies, waits for them, and re-layouts  5.41 us (4%)
    pallas_call x1, Pallas kernels, body(): pl.pallas_call(functools.partial(step_kernel, seq_count, batch_count, gra...  142 us
    unnamed x7, local copies, waits for them, and re-layouts  5.41 us

profile of v2, /device:TPU:0, one launch (start us, length us, event | category | flops | bytes accessed | tf_op | source)
XLA Modules:
  0.0 148.5 jit_solution(17119959551392383019)
XLA Ops:
  0.6 142.4 %shard_map.58 = (bf16[512,1024]{1,0:T(8,128)(2,1)}, bf16[512,2048]{1,0:T(8,128)(2,1)}, f32[256,3072]{1,0:T(8,128)}) custom-call(bf16[512,2048]{1,0:T(8,128)(2,1)} %bitcast.4, bf16[2048,3072]{1,0:T(8,128)(2,1)} %w_hbm.1, bf16[512,1024]{1,0:T(8,128)(2,1)} %bitcast.7), custom_call_target="tpu_custom_call" | custom-call | tf_op jit(solution)/shard_map/pallas_call | solution.py:758
  143.0 0.0 copy-start.1
  143.0 0.0 copy-start
  143.1 2.4 %copy.9 = bf16[1,512,1024]{2,1,0:T(8,128)(2,1)} copy(bf16[1,512,1024]{2,1,0:T(8,128)(2,1)} %bitcast.6) | data formatting | bytes 2097152
  145.5 0.0 copy-done.1
  145.5 1.3 copy.10
  146.8 0.0 copy-done
  146.8 1.7 %copy.11 = f32[256,3072]{1,0:T(8,128)} copy(f32[256,3072]{1,0:T(8,128)S(1)} %copy-done) | data formatting | bytes 6291456
Async XLA Ops:
  143.0 2.4 %copy-start.1 = (bf16[512,2048]{1,0:T(8,128)(2,1)S(1)}, bf16[512,2048]{1,0:T(8,128)(2,1)}, u32[]{:S(2)}) copy-start(bf16[512,2048]{1,0:T(8,128)(2,1)} %get-tuple-element.7) | copy-start | bytes 6291460
  143.0 3.7 %copy-start = (f32[256,3072]{1,0:T(8,128)S(1)}, f32[256,3072]{1,0:T(8,128)}, u32[]{:S(2)}) copy-start(f32[256,3072]{1,0:T(8,128)} %get-tuple-element.14) | copy-start | bytes 9437188

commit v3 on v2

--- a/solution.py
+++ b/solution.py
@@ -21,7 +21,7 @@
 SPLIT = {10: 2, 11: 2}
 EARLY = 4
 EARLY_LAGS = (1, 2, 3)
-MID_LAGS = (0, 1, 2)
+MID_LAGS = (0, 1, 3)
 LAST_LAGS = (0, 2, 4)
 
 
@@ -575,7 +575,7 @@
             late = EARLY_LAGS if position < EARLY else (MID_LAGS if unit.count == 1 else LAST_LAGS)
             for number, (stage, lag) in enumerate(zip((gather, close, take), late)):
                 events.setdefault(position + bits + lag, []).append(
-                    (1, -number, order, functools.partial(stage, unit))
+                    (1, number, order, functools.partial(stage, unit))
                 )
 
     def run_events(slot):
@@ -608,9 +608,11 @@
     chain(1)
     for index in range(2):
         w_tile(index).start()
-    for group in (2, 3):
-        project(group)
-        make_states(group)
+    project(2)
+    make_states(2)
+    project(3)
+    run_events(0)
+    make_states(3)
     chain(2, 1)
     chain(3, 1)
     ahead = {
@@ -638,7 +640,8 @@
     for slot in range(max(max(events), max(after)) + 1):
         for task in ahead.get(slot, []):
             task()
-        run_events(slot)
+        if slot:
+            run_events(slot)
         for position in opens.get(slot, [slot + 2]):
             if position < len(places):
                 open_place(position)

time: 149 us -> 146 us (0.980)
  Pallas kernels: 142 us -> 140 us
    pallas_call x1, Pallas kernels: 142 us -> 140 us  [body(): pl.pallas_call(functools.partial(step_kernel, seq_count, batch_count, gra...]
where the time goes in v3:
time: 146 us
  Pallas kernels  140 us (96%)
  local copies, waits for them, and re-layouts  5.41 us (4%)
    pallas_call x1, Pallas kernels, body(): pl.pallas_call(functools.partial(step_kernel, seq_count, batch_count, gra...  140 us
    unnamed x7, local copies, waits for them, and re-layouts  5.41 us

profile of v3, /device:TPU:0, one launch (start us, length us, event | category | flops | bytes accessed | tf_op | source)
XLA Modules:
  0.0 146.3 jit_solution(11408288941838098012)
XLA Ops:
  0.6 140.2 %shard_map.58 = (bf16[512,1024]{1,0:T(8,128)(2,1)}, bf16[512,2048]{1,0:T(8,128)(2,1)}, f32[256,3072]{1,0:T(8,128)}) custom-call(bf16[512,2048]{1,0:T(8,128)(2,1)} %bitcast.4, bf16[2048,3072]{1,0:T(8,128)(2,1)} %w_hbm.1, bf16[512,1024]{1,0:T(8,128)(2,1)} %bitcast.7), custom_call_target="tpu_custom_call" | custom-call | tf_op jit(solution)/shard_map/pallas_call | solution.py:761
  140.9 0.0 copy-start.1
  140.9 0.0 copy-start
  140.9 2.4 %copy.9 = bf16[1,512,1024]{2,1,0:T(8,128)(2,1)} copy(bf16[1,512,1024]{2,1,0:T(8,128)(2,1)} %bitcast.6) | data formatting | bytes 2097152
  143.3 0.0 copy-done.1
  143.3 1.3 copy.10
  144.6 0.0 copy-done
  144.6 1.7 %copy.11 = f32[256,3072]{1,0:T(8,128)} copy(f32[256,3072]{1,0:T(8,128)S(1)} %copy-done) | data formatting | bytes 6291456
Async XLA Ops:
  140.9 2.4 %copy-start.1 = (bf16[512,2048]{1,0:T(8,128)(2,1)S(1)}, bf16[512,2048]{1,0:T(8,128)(2,1)}, u32[]{:S(2)}) copy-start(bf16[512,2048]{1,0:T(8,128)(2,1)} %get-tuple-element.7) | copy-start | bytes 6291460
  140.9 3.7 %copy-start = (f32[256,3072]{1,0:T(8,128)S(1)}, f32[256,3072]{1,0:T(8,128)}, u32[]{:S(2)}) copy-start(f32[256,3072]{1,0:T(8,128)} %get-tuple-element.14) | copy-start | bytes 9437188

commit v4 on v3

--- a/solution.py
+++ b/solution.py
@@ -20,9 +20,9 @@
 PLACES = 6
 SPLIT = {10: 2, 11: 2}
 EARLY = 4
-EARLY_LAGS = (1, 2, 3)
+EARLY_LAGS = (1, 2, 4)
 MID_LAGS = (0, 1, 3)
-LAST_LAGS = (0, 2, 4)
+LAST_LAGS = (0, 2, 5)
 
 
 def bits_of(count):

time: 146 us -> 146 us (level)
  no operation moved by 1% of the time
where the time goes in v4:
time: 146 us
  Pallas kernels  140 us (96%)
  local copies, waits for them, and re-layouts  5.41 us (4%)
    pallas_call x1, Pallas kernels, body(): pl.pallas_call(functools.partial(step_kernel, seq_count, batch_count, gra...  140 us
    unnamed x7, local copies, waits for them, and re-layouts  5.41 us

profile of v4, /device:TPU:0, one launch (start us, length us, event | category | flops | bytes accessed | tf_op | source)
XLA Modules:
  0.0 146.3 jit_solution(14728877720132016431)
XLA Ops:
  0.6 140.2 %shard_map.58 = (bf16[512,1024]{1,0:T(8,128)(2,1)}, bf16[512,2048]{1,0:T(8,128)(2,1)}, f32[256,3072]{1,0:T(8,128)}) custom-call(bf16[512,2048]{1,0:T(8,128)(2,1)} %bitcast.4, bf16[2048,3072]{1,0:T(8,128)(2,1)} %w_hbm.1, bf16[512,1024]{1,0:T(8,128)(2,1)} %bitcast.7), custom_call_target="tpu_custom_call" | custom-call | tf_op jit(solution)/shard_map/pallas_call | solution.py:761
  140.9 0.0 copy-start.1
  140.9 0.0 copy-start
  140.9 2.4 %copy.9 = bf16[1,512,1024]{2,1,0:T(8,128)(2,1)} copy(bf16[1,512,1024]{2,1,0:T(8,128)(2,1)} %bitcast.6) | data formatting | bytes 2097152
  143.3 0.0 copy-done.1
  143.3 1.3 copy.10
  144.6 0.0 copy-done
  144.6 1.7 %copy.11 = f32[256,3072]{1,0:T(8,128)} copy(f32[256,3072]{1,0:T(8,128)S(1)} %copy-done) | data formatting | bytes 6291456
Async XLA Ops:
  140.9 2.4 %copy-start.1 = (bf16[512,2048]{1,0:T(8,128)(2,1)S(1)}, bf16[512,2048]{1,0:T(8,128)(2,1)}, u32[]{:S(2)}) copy-start(bf16[512,2048]{1,0:T(8,128)(2,1)} %get-tuple-element.7) | copy-start | bytes 6291460
  140.9 3.7 %copy-start = (f32[256,3072]{1,0:T(8,128)S(1)}, f32[256,3072]{1,0:T(8,128)}, u32[]{:S(2)}) copy-start(f32[256,3072]{1,0:T(8,128)} %get-tuple-element.14) | copy-start | bytes 9437188
